TPU v7x, 128 devices: a whole 4x4x4 slice. The times are simulated.
128 devices in a mesh: stn: 8 (over x_hi, y), tm: 16 (over x_lo, z, core).
Axes of the slice: x: 4 (x_hi: 2, x_lo: 2; x = x_hi * 2 + x_lo), y: 4, z: 4, core: 2. Of those that a mesh axis runs over, the one named last changes fastest.
Arguments:
- voltages: bfloat16 [512, 256, 4096], P('stn', 'tm'), may hold values from -52 to 52
- pfb_taps: float32 [16, 4096], replicated, may hold values from -1.5 to 1.5
- eq_gains: float32 [512, 2048], P('stn'), may hold values from 0.5 to 11
Outputs:
- visibilities: float32 [2048, 512, 512], P(('stn', 'tm'))
All inputs are finite; a program needn't handle non-finite values.
Results may differ from a plain program's by a relative error of at most 0.0014.
Values may be sent and summed in bfloat16 or wider, within the bound.
No kernel may reach another device: no remote copies, remote signals or barrier semaphores. Data moves between devices by JAX's collectives and lax.ppermute only.
A program may use at most 448 MiB of HBM per device.

v0:
```python
import math
import jax
import jax.numpy as jnp
from jax import lax
from jax.sharding import PartitionSpec as P


def from_behind(value, axis, steps):
    count = lax.axis_size(axis)
    first, last = (max(0, -steps), min(count, count - steps))
    return lax.ppermute(value, axis, [(source, source + steps) for source in range(first, last)])


def cos_sin(numer, denom):
    angle = 2.0 * math.pi / denom * (numer % denom).astype(jnp.float32)
    return (jnp.cos(angle), jnp.sin(angle))


def transform(filtered, channels):
    inputs_dev, frames_dev, length = filtered.shape
    inner_len = 64
    outer_len = length // inner_len
    kept_upper = channels // outer_len
    row_count = inputs_dev * frames_dev
    highest = lax.Precision.HIGHEST
    arranged = filtered.reshape(row_count, outer_len, inner_len)
    freq_one = lax.broadcasted_iota(jnp.int32, (outer_len, outer_len), 0)
    time_one = lax.broadcasted_iota(jnp.int32, (outer_len, outer_len), 1)
    cos_one, sin_one = cos_sin(freq_one * time_one, outer_len)
    section_one = jnp.stack([cos_one, -sin_one])
    partial_ft = jnp.einsum("qka,Rab->qkbR", section_one, arranged, precision=highest)
    freq_twist = lax.broadcasted_iota(jnp.int32, (outer_len, inner_len), 0)
    time_twist = lax.broadcasted_iota(jnp.int32, (outer_len, inner_len), 1)
    twist_cos, twist_sin = cos_sin(freq_twist * time_twist, length)
    twist_table = jnp.stack([jnp.stack([twist_cos, twist_sin]), jnp.stack([-twist_sin, twist_cos])])
    freq_two = lax.broadcasted_iota(jnp.int32, (kept_upper, inner_len), 0)
    time_two = lax.broadcasted_iota(jnp.int32, (kept_upper, inner_len), 1)
    cos_two, sin_two = cos_sin(freq_two * time_two, inner_len)
    section_two = jnp.stack(
        [jnp.stack([cos_two, sin_two], axis=1), jnp.stack([-sin_two, cos_two], axis=1)]
    )
    combined = jnp.einsum("qjrb,rskb->qjksb", section_two, twist_table, precision=highest)
    spectrum = jnp.einsum("qjksb,skbR->qjkR", combined, partial_ft, precision=highest)
    return spectrum.reshape(2, channels, row_count)


def per_device(voltages, pfb_taps, eq_gains):
    tap_count = pfb_taps.shape[0]
    history_len = tap_count - 1
    inputs_dev, frames_dev, length = voltages.shape
    channels = eq_gains.shape[1]
    station_groups = lax.axis_size("stn")
    time_groups = lax.axis_size("tm")
    per_group = channels // (station_groups * time_groups)
    all_inputs = inputs_dev * station_groups
    all_frames = frames_dev * time_groups
    earlier = from_behind(voltages[:, frames_dev - history_len :, :], "tm", 1)
    extended = jnp.concatenate([earlier, voltages], axis=1).astype(jnp.float32)
    kernel = jnp.flip(pfb_taps, axis=0)[:, None, :]
    filtered = lax.conv_general_dilated(
        extended,
        kernel,
        (1,),
        "VALID",
        dimension_numbers=("NWC", "WIO", "NWC"),
        feature_group_count=length,
        precision=lax.Precision.HIGHEST,
    )
    spectrum = transform(filtered, channels)
    gains_turned = jnp.transpose(eq_gains)
    spectra = (
        spectrum.reshape(2, channels, inputs_dev, frames_dev) * gains_turned[None, :, :, None]
    ).astype(jnp.bfloat16)
    shaped = spectra.reshape(2, station_groups * time_groups, per_group, inputs_dev * frames_dev)
    turned = lax.all_to_all(shaped, ("stn", "tm"), split_axis=1, concat_axis=1, tiled=True)
    blocks = turned.reshape(2, station_groups, time_groups, per_group, inputs_dev, frames_dev)
    columns = jnp.transpose(blocks, (0, 3, 1, 4, 2, 5)).reshape(
        2, per_group, all_inputs, all_frames
    )
    swapped = jnp.stack([columns[1], -columns[0]])
    vis_real = jnp.einsum("rcnt,rcmt->cnm", columns, columns, preferred_element_type=jnp.float32)
    vis_imag = jnp.einsum("rcnt,rcmt->cnm", swapped, columns, preferred_element_type=jnp.float32)
    local_power = jnp.sum(jnp.diagonal(vis_real, axis1=1, axis2=2), axis=0)
    power = lax.psum(local_power, ("stn", "tm"))
    scale = lax.rsqrt(power / (all_frames * channels) + 1e-06)
    weight = scale[:, None] * scale[None, :] / all_frames
    row_ids = lax.broadcasted_iota(jnp.int32, (all_inputs, all_inputs), 0)
    col_ids = lax.broadcasted_iota(jnp.int32, (all_inputs, all_inputs), 1)
    lower = row_ids >= col_ids
    return jnp.where(lower[None], vis_real, vis_imag) * weight[None]


def solution(mesh):
    in_specs = (P("stn", "tm", None), P(), P("stn", None))
    out_specs = P(("stn", "tm"), None, None)
    return jax.shard_map(
        per_device, mesh=mesh, in_specs=in_specs, out_specs=out_specs, check_vma=False
    )
```

profile of v0, /device:TPU:1, one launch (start us, length us, event | category | flops | bytes accessed | tf_op | source)
XLA Modules:
  0.0 891.8 jit_solution(8095447733145545676)
XLA Ops:
  0.0 11.4 %copy.46 = bf16[64,16,4096]{2,0,1:T(8,128)(2,1)} copy(bf16[64,16,4096]{2,1,0:T(8,128)(2,1)} %param.3) | data formatting | bytes 16777216 | tf_op args[0]
  11.4 7.4 slice.19
  18.8 5.1 collective-permute-start
  23.8 0.1 fusion.37
  24.0 0.1 fusion.33
  24.2 0.1 copy.70
  24.3 0.1 fusion.40
  24.4 0.1 fusion.38
  24.5 0.1 copy.71
  24.7 5.3 convolution_bitcast_fusion.2
  29.9 6.8 copy.54
  36.7 0.5 rev.4
  37.2 0.3 copy.56
  37.6 21.5 %mul.180 = f32[2048,64,16]{2,1,0:T(8,128)} broadcast(f32[2048,64]{1,0:T(8,128)S(1)} %copy.56), dimensions={0,1} | broadcast | bytes 8912896 | tf_op jit(solution)/shard_map/mul | solution.py:72
  59.0 54.5 %mul.181 = f32[128,16,1024]{2,1,0:T(8,128)} reshape(f32[2048,64,16]{2,1,0:T(8,128)} %mul.180) | data formatting | bytes 16777216 | tf_op jit(solution)/shard_map/mul | solution.py:72
  113.5 0.8 sine_negate_fusion
  114.3 0.0 collective-permute-done
  114.3 22.0 %fusion.3 = f32[64,16,4096]{2,0,1:T(8,128)S(1)} fusion(bf16[64,16,4096]{2,0,1:T(8,128)(2,1)} %copy.46, bf16[64,15,4096]{2,0,1:T(8,128)(2,1)} %collective-permute-done, f32[16,1,4096]{2,0,1:T(8,128)S(1)} %bitcast.69), kind=kOutput, calls=%fused_computation.6 | convolution fusion | flops 813432832 | bytes 33292288 | tf_op jit(solution)/shard_map/conv_general_dilated | solution.py:60
  136.4 18.8 %copy.49 = f32[64,16,4096]{2,1,0:T(8,128)} copy(f32[64,16,4096]{2,0,1:T(8,128)S(1)} %fusion.3) | data formatting | bytes 33554432 | tf_op jit(solution)/shard_map/conv_general_dilated | solution.py:60
  155.2 27.0 %reshape.234 = f32[1024,64,64]{2,1,0:T(8,128)} reshape(f32[64,16,4096]{2,1,0:T(8,128)} %copy.49) | data formatting | bytes 33554432 | tf_op jit(solution)/shard_map/reshape | solution.py:26
  182.2 26.2 %copy.69 = f32[1024,64,64,1]{0,1,3,2:T(8,128)} copy(f32[1024,64,64,1]{2,1,0,3:T(8,128)} %bitcast.62) | data formatting | bytes 33554432 | tf_op jit(solution)/shard_map/reshape | solution.py:26
  208.4 33.7 %convolution_bitcast_fusion = f32[2,64,64,1024,1]{3,1,0,2,4:T(8,128)} fusion(f32[1024,64,64,1]{0,1,3,2:T(8,128)} %copy.69, f32[1,64,64]{2,1,0:T(8,128)S(1)} %copy-done.5, f32[1,64,64]{2,1,0:T(8,128)S(1)} %copy-done.6), kind=kOutput, calls=%fused_computation.10 | convolution fusion | flops 6442459136 | bytes 50364416 | tf_op jit(solution)/shard_map/qka,Rab->qkbR/dot_general | solution.py:31
  242.1 47.6 %fusion.7 = f32[2,32,64,1024]{3,1,0,2:T(8,128)} fusion(f32[2,32,64,2,64]{4,1,3,0,2:T(8,128)S(1)} %copy-done.1, f32[2,64,64,1024,1]{3,1,0,2,4:T(8,128)} %convolution_bitcast_fusion), kind=kOutput, calls=%fused_computation.11 | convolution fusion | flops 6442450944 | bytes 52428800 | tf_op jit(solution)/shard_map/qjksb,skbR->qjkR/dot_general | solution.py:43
  289.7 15.6 %copy.55 = f32[2,32,64,1024]{3,2,1,0:T(8,128)S(1)} copy(f32[2,32,64,1024]{3,1,0,2:T(8,128)} %fusion.7) | data formatting | bytes 33554432 | tf_op jit(solution)/shard_map/qjksb,skbR->qjkR/transpose | solution.py:43
  305.3 5.1 multiply_convert_fusion
  310.5 8.5 copy.57
  319.0 10.1 %all-to-all-start = ((bf16[2,128,16,1024]{3,2,0,1:T(8,128)(2,1)}), bf16[2,128,16,1024]{3,2,0,1:T(8,128)(2,1)}, u32[]{:S(2)}, u32[]{:S(2)}) async-start(bf16[2,128,16,1024]{3,2,0,1:T(8,128)(2,1)} %copy.57), calls=%async_computation | async-start | bytes 16777216 | tf_op jit(solution)/shard_map/all_to_all | solution.py:75
  329.1 0.5 shift-left_or_fusion
  329.6 0.8 iota_compare_fusion
  330.4 100.1 %all-to-all-done = bf16[2,128,16,1024]{3,2,0,1:T(8,128)(2,1)} async-done(((bf16[2,128,16,1024]{3,2,0,1:T(8,128)(2,1)}), bf16[2,128,16,1024]{3,2,0,1:T(8,128)(2,1)}, u32[]{:S(2)}, u32[]{:S(2)}) %all-to-all-start) | async-done | bytes 8388640 | tf_op jit(solution)/shard_map/all_to_all | solution.py:75
  430.5 62.1 %reshape.251 = bf16[2,8,16,16,64,16]{5,4,3,0,2,1:T(8,128)(2,1)} reshape(bf16[2,128,16,1024]{3,2,0,1:T(8,128)(2,1)} %all-to-all-done) | data formatting | bytes 16777216 | tf_op jit(solution)/shard_map/reshape | solution.py:76
  492.6 56.9 %copy.59 = bf16[2,8,16,16,64,16]{4,5,2,1,3,0:T(8,128)(2,1)} copy(bf16[2,8,16,16,64,16]{5,4,3,0,2,1:T(8,128)(2,1)} %reshape.251) | data formatting | bytes 16777216 | tf_op jit(solution)/shard_map/reshape | solution.py:76
  549.5 57.9 %copy.60 = bf16[2,16,8,64,16,16]{3,2,5,4,1,0:T(8,128)(2,1)} copy(bf16[2,16,8,64,16,16]{5,3,1,0,4,2:T(8,128)(2,1)} %bitcast.18) | data formatting | bytes 16777216 | tf_op jit(solution)/shard_map/transpose | solution.py:77
  607.4 22.5 %reshape.236 = bf16[2,16,512,256]{2,3,1,0:T(8,128)(2,1)} reshape(bf16[2,16,8,64,16,16]{3,2,5,4,1,0:T(8,128)(2,1)} %copy.60) | data formatting | bytes 16777216 | tf_op jit(solution)/shard_map/reshape | solution.py:77
  629.9 16.5 %convolution_bitcast_fusion.1 = f32[16,512,512]{2,1,0:T(8,128)} fusion(bf16[2,16,512,256]{2,3,1,0:T(8,128)(2,1)} %reshape.236), kind=kOutput, calls=%fused_computation.12 | convolution fusion | flops 4294967296 | bytes 25165824 | tf_op jit(solution)/shard_map/rcnt,rcmt->cnm/dot_general | solution.py:81
  646.3 11.7 %fusion.44 = (bf16[1,16,8,64,16,16]{3,5,4,2,1,0:T(8,128)(2,1)}, bf16[1,16,8,64,16,16]{3,5,4,2,1,0:T(8,128)(2,1)}) fusion(bf16[2,16,8,64,16,16]{3,5,4,2,1,0:T(8,128)(2,1)} %bitcast.63), kind=kLoop, calls=%fused_computation.70 | loop fusion | flops 2097152 | bytes 16777216 | tf_op jit(solution)/shard_map/slice | solution.py:80
  658.0 20.2 %copy.64 = bf16[1,16,8,64,16,16]{3,2,5,4,1,0:T(8,128)(2,1)} copy(bf16[1,16,8,64,16,16]{3,5,4,2,1,0:T(8,128)(2,1)} %get-tuple-element.6) | data formatting | bytes 8388608 | tf_op jit(solution)/shard_map/neg | solution.py:80
  678.2 11.8 %neg.47 = bf16[1,16,512,256]{2,3,1,0:T(8,128)(2,1)} reshape(bf16[1,16,8,64,16,16]{3,2,5,4,1,0:T(8,128)(2,1)} %copy.64) | data formatting | bytes 8388608 | tf_op jit(solution)/shard_map/neg | solution.py:80
  690.1 6.3 copy.66
  696.4 20.2 %copy.63 = bf16[1,16,8,64,16,16]{3,2,5,4,1,0:T(8,128)(2,1)} copy(bf16[1,16,8,64,16,16]{3,5,4,2,1,0:T(8,128)(2,1)} %get-tuple-element.5) | data formatting | bytes 8388608 | tf_op jit(solution)/shard_map/slice | solution.py:80
  716.6 11.8 %slice.15 = bf16[1,16,512,256]{2,3,1,0:T(8,128)(2,1)} reshape(bf16[1,16,8,64,16,16]{3,2,5,4,1,0:T(8,128)(2,1)} %copy.63) | data formatting | bytes 8388608 | tf_op jit(solution)/shard_map/slice | solution.py:80
  728.4 6.3 copy.65
  734.8 62.4 %copy.68 = f32[16,512,512]{0,2,1:T(8,128)} copy(f32[16,512,512]{2,1,0:T(8,128)} %convolution_bitcast_fusion.1) | data formatting | bytes 33554432 | tf_op jit(solution)/shard_map/rcnt,rcmt->cnm/dot_general | solution.py:81
  797.1 5.5 gather_fusion
  802.6 0.1 reduce_sum.9
  802.8 69.5 %psum.7 = f32[512]{0:T(512)S(1)} all-reduce(f32[512]{0:T(512)S(1)} %reduce_sum.9), channel_id=1, replica_groups=mesh['stn'=8,'tm'=16] {'stn','tm'}, use_global_device_ids=true, to_apply=%region_1.2 | all-reduce | flops 512 | bytes 4096 | tf_op jit(solution)/shard_map/psum | solution.py:84
  872.3 0.1 multiply_multiply_fusion
  872.5 18.9 %fusion.2 = f32[16,512,512]{2,1,0:T(8,128)} fusion(f32[16,512,512]{2,1,0:T(8,128)} %convolution_bitcast_fusion.1, bf16[1,16,512,256]{3,2,0,1:T(8,128)(2,1)} %copy.66, bf16[1,16,512,256]{3,2,0,1:T(8,128)(2,1)} %copy.65, bf16[2,16,512,256]{2,3,1,0:T(8,128)(2,1)} %reshape.236, f32[512,512]{1,0:T(8,128)S(1)} %multiply_multiply_fusion, ...), kind=kOutput, calls=%fused_computation.4 | convolution fusion | flops 4307550208 | bytes 51642368 | tf_op jit(solution)/shard_map/rcnt,rcmt->cnm/dot_general | solution.py:82
  (24 shorter events, 0.1 us)
Async XLA Ops:
  18.8 18.0 %copy-start.4 = (f32[16,4096]{1,0:T(8,128)S(1)}, f32[16,4096]{1,0:T(8,128)}, u32[]{:S(2)}) copy-start(f32[16,4096]{1,0:T(8,128)} %param.4) | copy-start | bytes 786436
  18.8 18.5 %copy-start.3 = (f32[64,2048]{1,0:T(8,128)S(1)}, f32[64,2048]{1,0:T(8,128)}, u32[]{:S(2)}) copy-start(f32[64,2048]{1,0:T(8,128)} %param.5) | copy-start | bytes 1572868
  18.8 95.6 %collective-permute-start = (bf16[64,15,4096]{2,0,1:T(8,128)(2,1)}, bf16[64,15,4096]{2,0,1:T(8,128)(2,1)}, u32[]{:S(2)}, u32[]{:S(2)}) collective-permute-start(bf16[64,15,4096]{2,0,1:T(8,128)(2,1)} %slice.19), channel_id=1, source_target_pairs={{0,1},{1,2},{2,3},{3,4},{4,5},{5,6},{6,7},{7,8},{8,9},{9,10},{10,1... | collective-permute-start | bytes 23592968 | tf_op jit(solution)/shard_map/ppermute | solution.py:11
  182.2 26.2 %copy-start.5 = (f32[1,64,64]{2,1,0:T(8,128)S(1)}, f32[1,64,64]{2,1,0:T(8,128)}, u32[]{:S(2)}) copy-start(f32[1,64,64]{2,1,0:T(8,128)} %get-tuple-element.15) | copy-start | bytes 49156
  182.2 26.2 %copy-start.6 = (f32[1,64,64]{2,1,0:T(8,128)S(1)}, f32[1,64,64]{2,1,0:T(8,128)}, u32[]{:S(2)}) copy-start(f32[1,64,64]{2,1,0:T(8,128)} %get-tuple-element.16) | copy-start | bytes 49156
  208.4 33.7 %copy-start.1 = (f32[2,32,64,2,64]{4,1,3,0,2:T(8,128)S(1)}, f32[2,32,64,2,64]{4,1,3,0,2:T(8,128)}, u32[]{:S(2)}) copy-start(f32[2,32,64,2,64]{4,1,3,0,2:T(8,128)} %copy.54) | copy-start | bytes 6291460
  208.4 96.9 %slice-start = ((s8[8388608]{0:T(1024)(128)(4,1)}), s8[4194304]{0:T(1024)(128)(4,1)S(1)}, s32[]{:S(2)}) async-start(s8[8388608]{0:T(1024)(128)(4,1)} %bitcast.66), calls=%async_computation.1 | async-start | bytes 8388608
  242.1 63.2 %slice-start.1 = ((s8[8388608]{0:T(1024)(128)(4,1)}), s8[4194304]{0:T(1024)(128)(4,1)S(1)}, s32[]{:S(2)}) async-start(s8[8388608]{0:T(1024)(128)(4,1)} %bitcast.66), calls=%async_computation.2 | async-start | bytes 8388608
  319.0 111.6 %all-to-all-start = ((bf16[2,128,16,1024]{3,2,0,1:T(8,128)(2,1)}), bf16[2,128,16,1024]{3,2,0,1:T(8,128)(2,1)}, u32[]{:S(2)}, u32[]{:S(2)}) async-start(bf16[2,128,16,1024]{3,2,0,1:T(8,128)(2,1)} %copy.57), calls=%async_computation | async-start | bytes 16777216 | tf_op jit(solution)/shard_map/all_to_all | solution.py:75
  734.8 62.4 %copy-start = (s32[512,1]{0,1:T(1,128)S(1)}, s32[512,1]{0,1:T(1,128)}, u32[]{:S(2)}) copy-start(s32[512,1]{0,1:T(1,128)} %shift-left_or_fusion) | copy-start | bytes 6148
  734.8 137.7 %copy-start.2 = (pred[512,512]{1,0:T(8,128)(4,1)S(1)}, pred[512,512]{1,0:T(8,128)(4,1)}, u32[]{:S(2)}) copy-start(pred[512,512]{1,0:T(8,128)(4,1)} %iota_compare_fusion) | copy-start | bytes 786436
where the time goes:
time: 907 us; the launch traced here: 892 us
  local copies, waits for them, and re-layouts  543 us (60%)
  matrix products  144 us (16%)
  waiting for transfers between devices  100 us (11%)
  blocking collectives  69.5 us (8%)
  other arithmetic  19.7 us (2%)
  starting transfers between devices  15.2 us (2%)
    reshape x2, local copies, waits for them, and re-layouts, per_device(): turned.reshape(2, station_groups, time_groups, per_group, inputs_dev, fra...  119 us
    all_to_all x1, waiting for transfers between devices, per_device(): lax.all_to_all(shaped, ('stn', 'tm'), split_axis=1, concat_axis=1, tiled=...  100 us
    mul x2, local copies, waits for them, and re-layouts, per_device(): spectrum.reshape(2, channels, inputs_dev, frames_dev)  76 us
    psum x1, blocking collectives, per_device(): power = lax.psum(local_power, ('stn', 'tm'))  69.5 us
    dot_general x1, local copies, waits for them, and re-layouts, per_device(): jnp.einsum('rcnt,rcmt->cnm', columns, columns, preferred_element_type=jnp...  62.4 us
    transpose x1, local copies, waits for them, and re-layouts, per_device(): jnp.transpose(blocks, (0, 3, 1, 4, 2, 5))  57.9 us
    reshape x2, local copies, waits for them, and re-layouts, transform(): arranged = filtered.reshape(row_count, outer_len, inner_len)  53.2 us
    dot_general x1, matrix products, transform(): jnp.einsum('qjksb,skbR->qjkR', combined, partial_ft, precision=highest)  47.6 us
  transfers between devices with their start and end apart: 2, of which 1 were waited for; matrix products, arithmetic and copies ran while one was open for 10% of the time, Pallas kernels for 0%

commit v1 on v0

--- a/solution.py
+++ b/solution.py
@@ -81,7 +81,7 @@
     vis_real = jnp.einsum("rcnt,rcmt->cnm", columns, columns, preferred_element_type=jnp.float32)
     vis_imag = jnp.einsum("rcnt,rcmt->cnm", swapped, columns, preferred_element_type=jnp.float32)
     local_power = jnp.sum(jnp.diagonal(vis_real, axis1=1, axis2=2), axis=0)
-    power = lax.psum(local_power, ("stn", "tm"))
+    power = jnp.sum(lax.all_gather(local_power, ("stn", "tm")), axis=0)
     scale = lax.rsqrt(power / (all_frames * channels) + 1e-06)
     weight = scale[:, None] * scale[None, :] / all_frames
     row_ids = lax.broadcasted_iota(jnp.int32, (all_inputs, all_inputs), 0)

time: 907 us -> 1020 us (1.12)
  blocking collectives: 69.5 us -> 179 us
    all_gather x0 -> x1, blocking collectives: none -> 179 us  [per_device(): power = jnp.sum(lax.all_gather(local_power, ('stn', 'tm')), axis=0)]
    psum x1 -> x0, blocking collectives: 69.5 us -> none  [per_device(): power = lax.psum(local_power, ('stn', 'tm'))]
  transfers between devices with their start and end apart: 2 -> 2, of which waited for: 1 -> 1; matrix products, arithmetic and copies ran while one was open for 10% -> 9% of each run, Pallas kernels for 0% -> 0%
where the time goes in v1:
time: 1020 us; the launch traced here: 1000 us
  local copies, waits for them, and re-layouts  543 us (53%)
  blocking collectives  179 us (18%)
  matrix products  144 us (14%)
  waiting for transfers between devices  100 us (10%)
  other arithmetic  19.9 us (2%)
  starting transfers between devices  15.2 us (1%)
    all_gather x1, blocking collectives, per_device(): power = jnp.sum(lax.all_gather(local_power, ('stn', 'tm')), axis=0)  179 us
    reshape x2, local copies, waits for them, and re-layouts, per_device(): turned.reshape(2, station_groups, time_groups, per_group, inputs_dev, fra...  119 us
    all_to_all x1, waiting for transfers between devices, per_device(): lax.all_to_all(shaped, ('stn', 'tm'), split_axis=1, concat_axis=1, tiled=...  100 us
    mul x2, local copies, waits for them, and re-layouts, per_device(): spectrum.reshape(2, channels, inputs_dev, frames_dev)  76 us
    dot_general x1, local copies, waits for them, and re-layouts, per_device(): jnp.einsum('rcnt,rcmt->cnm', columns, columns, preferred_element_type=jnp...  62.4 us
    transpose x1, local copies, waits for them, and re-layouts, per_device(): jnp.transpose(blocks, (0, 3, 1, 4, 2, 5))  57.9 us
    reshape x2, local copies, waits for them, and re-layouts, transform(): arranged = filtered.reshape(row_count, outer_len, inner_len)  53.2 us
    dot_general x1, matrix products, transform(): jnp.einsum('qjksb,skbR->qjkR', combined, partial_ft, precision=highest)  47.6 us
  transfers between devices with their start and end apart: 2, of which 1 were waited for; matrix products, arithmetic and copies ran while one was open for 9% of the time, Pallas kernels for 0%

profile of v1, /device:TPU:1, one launch (start us, length us, event | category | flops | bytes accessed | tf_op | source)
XLA Modules:
  0.0 1001.9 jit_solution(6794327095498327392)
XLA Ops:
  0.0 11.4 %copy.46 = bf16[64,16,4096]{2,0,1:T(8,128)(2,1)} copy(bf16[64,16,4096]{2,1,0:T(8,128)(2,1)} %param.3) | data formatting | bytes 16777216 | tf_op args[0]
  11.4 7.4 slice.19
  18.8 5.1 collective-permute-start
  23.8 0.1 fusion.37
  24.0 0.1 fusion.33
  24.2 0.1 copy.70
  24.3 0.1 fusion.40
  24.4 0.1 fusion.38
  24.5 0.1 copy.71
  24.7 5.3 convolution_bitcast_fusion.2
  29.9 6.8 copy.54
  36.7 0.5 rev.4
  37.2 0.3 copy.56
  37.6 21.5 %mul.180 = f32[2048,64,16]{2,1,0:T(8,128)} broadcast(f32[2048,64]{1,0:T(8,128)S(1)} %copy.56), dimensions={0,1} | broadcast | bytes 8912896 | tf_op jit(solution)/shard_map/mul | solution.py:72
  59.0 54.5 %mul.181 = f32[128,16,1024]{2,1,0:T(8,128)} reshape(f32[2048,64,16]{2,1,0:T(8,128)} %mul.180) | data formatting | bytes 16777216 | tf_op jit(solution)/shard_map/mul | solution.py:72
  113.5 0.8 sine_negate_fusion
  114.3 22.0 %fusion.3 = f32[64,16,4096]{2,0,1:T(8,128)S(1)} fusion(bf16[64,16,4096]{2,0,1:T(8,128)(2,1)} %copy.46, bf16[64,15,4096]{2,0,1:T(8,128)(2,1)} %collective-permute-done, f32[16,1,4096]{2,0,1:T(8,128)S(1)} %bitcast.70), kind=kOutput, calls=%fused_computation.6 | convolution fusion | flops 813432832 | bytes 33292288 | tf_op jit(solution)/shard_map/conv_general_dilated | solution.py:60
  136.4 18.8 %copy.49 = f32[64,16,4096]{2,1,0:T(8,128)} copy(f32[64,16,4096]{2,0,1:T(8,128)S(1)} %fusion.3) | data formatting | bytes 33554432 | tf_op jit(solution)/shard_map/conv_general_dilated | solution.py:60
  155.2 27.0 %reshape.244 = f32[1024,64,64]{2,1,0:T(8,128)} reshape(f32[64,16,4096]{2,1,0:T(8,128)} %copy.49) | data formatting | bytes 33554432 | tf_op jit(solution)/shard_map/reshape | solution.py:26
  182.2 26.2 %copy.69 = f32[1024,64,64,1]{0,1,3,2:T(8,128)} copy(f32[1024,64,64,1]{2,1,0,3:T(8,128)} %bitcast.63) | data formatting | bytes 33554432 | tf_op jit(solution)/shard_map/reshape | solution.py:26
  208.4 33.7 %convolution_bitcast_fusion = f32[2,64,64,1024,1]{3,1,0,2,4:T(8,128)} fusion(f32[1024,64,64,1]{0,1,3,2:T(8,128)} %copy.69, f32[1,64,64]{2,1,0:T(8,128)S(1)} %copy-done.5, f32[1,64,64]{2,1,0:T(8,128)S(1)} %copy-done.6), kind=kOutput, calls=%fused_computation.10 | convolution fusion | flops 6442459136 | bytes 50364416 | tf_op jit(solution)/shard_map/qka,Rab->qkbR/dot_general | solution.py:31
  242.1 47.6 %fusion.7 = f32[2,32,64,1024]{3,1,0,2:T(8,128)} fusion(f32[2,32,64,2,64]{4,1,3,0,2:T(8,128)S(1)} %copy-done.1, f32[2,64,64,1024,1]{3,1,0,2,4:T(8,128)} %convolution_bitcast_fusion), kind=kOutput, calls=%fused_computation.11 | convolution fusion | flops 6442450944 | bytes 52428800 | tf_op jit(solution)/shard_map/qjksb,skbR->qjkR/dot_general | solution.py:43
  289.7 15.6 %copy.55 = f32[2,32,64,1024]{3,2,1,0:T(8,128)S(1)} copy(f32[2,32,64,1024]{3,1,0,2:T(8,128)} %fusion.7) | data formatting | bytes 33554432 | tf_op jit(solution)/shard_map/qjksb,skbR->qjkR/transpose | solution.py:43
  305.3 5.1 multiply_convert_fusion
  310.5 8.5 copy.57
  319.0 10.1 %all-to-all-start = ((bf16[2,128,16,1024]{3,2,0,1:T(8,128)(2,1)}), bf16[2,128,16,1024]{3,2,0,1:T(8,128)(2,1)}, u32[]{:S(2)}, u32[]{:S(2)}) async-start(bf16[2,128,16,1024]{3,2,0,1:T(8,128)(2,1)} %copy.57), calls=%async_computation | async-start | bytes 16777216 | tf_op jit(solution)/shard_map/all_to_all | solution.py:75
  329.1 0.5 shift-left_or_fusion
  329.6 0.8 iota_compare_fusion
  330.4 100.1 %all-to-all-done = bf16[2,128,16,1024]{3,2,0,1:T(8,128)(2,1)} async-done(((bf16[2,128,16,1024]{3,2,0,1:T(8,128)(2,1)}), bf16[2,128,16,1024]{3,2,0,1:T(8,128)(2,1)}, u32[]{:S(2)}, u32[]{:S(2)}) %all-to-all-start) | async-done | bytes 8388640 | tf_op jit(solution)/shard_map/all_to_all | solution.py:75
  430.5 62.1 %reshape.265 = bf16[2,8,16,16,64,16]{5,4,3,0,2,1:T(8,128)(2,1)} reshape(bf16[2,128,16,1024]{3,2,0,1:T(8,128)(2,1)} %all-to-all-done) | data formatting | bytes 16777216 | tf_op jit(solution)/shard_map/reshape | solution.py:76
  492.6 56.9 %copy.59 = bf16[2,8,16,16,64,16]{4,5,2,1,3,0:T(8,128)(2,1)} copy(bf16[2,8,16,16,64,16]{5,4,3,0,2,1:T(8,128)(2,1)} %reshape.265) | data formatting | bytes 16777216 | tf_op jit(solution)/shard_map/reshape | solution.py:76
  549.5 57.9 %copy.60 = bf16[2,16,8,64,16,16]{3,2,5,4,1,0:T(8,128)(2,1)} copy(bf16[2,16,8,64,16,16]{5,3,1,0,4,2:T(8,128)(2,1)} %bitcast.18) | data formatting | bytes 16777216 | tf_op jit(solution)/shard_map/transpose | solution.py:77
  607.4 22.5 %reshape.246 = bf16[2,16,512,256]{2,3,1,0:T(8,128)(2,1)} reshape(bf16[2,16,8,64,16,16]{3,2,5,4,1,0:T(8,128)(2,1)} %copy.60) | data formatting | bytes 16777216 | tf_op jit(solution)/shard_map/reshape | solution.py:77
  629.9 16.5 %convolution_bitcast_fusion.1 = f32[16,512,512]{2,1,0:T(8,128)} fusion(bf16[2,16,512,256]{2,3,1,0:T(8,128)(2,1)} %reshape.246), kind=kOutput, calls=%fused_computation.12 | convolution fusion | flops 4294967296 | bytes 25165824 | tf_op jit(solution)/shard_map/rcnt,rcmt->cnm/dot_general | solution.py:81
  646.3 11.7 %fusion.44 = (bf16[1,16,8,64,16,16]{3,5,4,2,1,0:T(8,128)(2,1)}, bf16[1,16,8,64,16,16]{3,5,4,2,1,0:T(8,128)(2,1)}) fusion(bf16[2,16,8,64,16,16]{3,5,4,2,1,0:T(8,128)(2,1)} %bitcast.64), kind=kLoop, calls=%fused_computation.70 | loop fusion | flops 2097152 | bytes 16777216 | tf_op jit(solution)/shard_map/slice | solution.py:80
  658.0 20.2 %copy.64 = bf16[1,16,8,64,16,16]{3,2,5,4,1,0:T(8,128)(2,1)} copy(bf16[1,16,8,64,16,16]{3,5,4,2,1,0:T(8,128)(2,1)} %get-tuple-element.6) | data formatting | bytes 8388608 | tf_op jit(solution)/shard_map/neg | solution.py:80
  678.2 11.8 %neg.47 = bf16[1,16,512,256]{2,3,1,0:T(8,128)(2,1)} reshape(bf16[1,16,8,64,16,16]{3,2,5,4,1,0:T(8,128)(2,1)} %copy.64) | data formatting | bytes 8388608 | tf_op jit(solution)/shard_map/neg | solution.py:80
  690.1 6.3 copy.66
  696.4 20.2 %copy.63 = bf16[1,16,8,64,16,16]{3,2,5,4,1,0:T(8,128)(2,1)} copy(bf16[1,16,8,64,16,16]{3,5,4,2,1,0:T(8,128)(2,1)} %get-tuple-element.5) | data formatting | bytes 8388608 | tf_op jit(solution)/shard_map/slice | solution.py:80
  716.6 11.8 %slice.15 = bf16[1,16,512,256]{2,3,1,0:T(8,128)(2,1)} reshape(bf16[1,16,8,64,16,16]{3,2,5,4,1,0:T(8,128)(2,1)} %copy.63) | data formatting | bytes 8388608 | tf_op jit(solution)/shard_map/slice | solution.py:80
  728.4 6.3 copy.65
  734.8 62.4 %copy.68 = f32[16,512,512]{0,2,1:T(8,128)} copy(f32[16,512,512]{2,1,0:T(8,128)} %convolution_bitcast_fusion.1) | data formatting | bytes 33554432 | tf_op jit(solution)/shard_map/rcnt,rcmt->cnm/dot_general | solution.py:81
  797.1 5.5 gather_fusion
  802.6 0.1 reduce_sum.18
  802.8 179.4 %all-gather.1 = f32[128,1,512]{2,1,0:T(1,128)S(1)} all-gather(f32[1,1,512]{2,1,0:T(1,128)S(1)} %bitcast.71), channel_id=2, replica_groups=mesh['stn'=8,'tm'=16] {'stn','tm'}, dimensions={0}, use_global_device_ids=true | all-gather | bytes 264192 | tf_op jit(solution)/shard_map/all_gather | solution.py:84
  982.2 0.2 reduce_sum.19
  982.4 0.1 multiply_multiply_fusion
  982.6 18.9 %fusion.2 = f32[16,512,512]{2,1,0:T(8,128)} fusion(f32[16,512,512]{2,1,0:T(8,128)} %convolution_bitcast_fusion.1, bf16[1,16,512,256]{3,2,0,1:T(8,128)(2,1)} %copy.66, bf16[1,16,512,256]{3,2,0,1:T(8,128)(2,1)} %copy.65, bf16[2,16,512,256]{2,3,1,0:T(8,128)(2,1)} %reshape.246, f32[512,512]{1,0:T(8,128)S(1)} %multiply_multiply_fusion, ...), kind=kOutput, calls=%fused_computation.4 | convolution fusion | flops 4307550208 | bytes 51642368 | tf_op jit(solution)/shard_map/rcnt,rcmt->cnm/dot_general | solution.py:82
  (25 shorter events, 0.1 us)
Async XLA Ops:
  18.8 18.0 %copy-start.4 = (f32[16,4096]{1,0:T(8,128)S(1)}, f32[16,4096]{1,0:T(8,128)}, u32[]{:S(2)}) copy-start(f32[16,4096]{1,0:T(8,128)} %param.4) | copy-start | bytes 786436
  18.8 18.5 %copy-start.3 = (f32[64,2048]{1,0:T(8,128)S(1)}, f32[64,2048]{1,0:T(8,128)}, u32[]{:S(2)}) copy-start(f32[64,2048]{1,0:T(8,128)} %param.5) | copy-start | bytes 1572868
  18.8 95.6 %collective-permute-start = (bf16[64,15,4096]{2,0,1:T(8,128)(2,1)}, bf16[64,15,4096]{2,0,1:T(8,128)(2,1)}, u32[]{:S(2)}, u32[]{:S(2)}) collective-permute-start(bf16[64,15,4096]{2,0,1:T(8,128)(2,1)} %slice.19), channel_id=1, source_target_pairs={{0,1},{1,2},{2,3},{3,4},{4,5},{5,6},{6,7},{7,8},{8,9},{9,10},{10,1... | collective-permute-start | bytes 23592968 | tf_op jit(solution)/shard_map/ppermute | solution.py:11
  182.2 26.2 %copy-start.5 = (f32[1,64,64]{2,1,0:T(8,128)S(1)}, f32[1,64,64]{2,1,0:T(8,128)}, u32[]{:S(2)}) copy-start(f32[1,64,64]{2,1,0:T(8,128)} %get-tuple-element.15) | copy-start | bytes 49156
  182.2 26.2 %copy-start.6 = (f32[1,64,64]{2,1,0:T(8,128)S(1)}, f32[1,64,64]{2,1,0:T(8,128)}, u32[]{:S(2)}) copy-start(f32[1,64,64]{2,1,0:T(8,128)} %get-tuple-element.16) | copy-start | bytes 49156
  208.4 33.7 %copy-start.1 = (f32[2,32,64,2,64]{4,1,3,0,2:T(8,128)S(1)}, f32[2,32,64,2,64]{4,1,3,0,2:T(8,128)}, u32[]{:S(2)}) copy-start(f32[2,32,64,2,64]{4,1,3,0,2:T(8,128)} %copy.54) | copy-start | bytes 6291460
  208.4 96.9 %slice-start = ((s8[8388608]{0:T(1024)(128)(4,1)}), s8[4194304]{0:T(1024)(128)(4,1)S(1)}, s32[]{:S(2)}) async-start(s8[8388608]{0:T(1024)(128)(4,1)} %bitcast.67), calls=%async_computation.1 | async-start | bytes 8388608
  242.1 63.2 %slice-start.1 = ((s8[8388608]{0:T(1024)(128)(4,1)}), s8[4194304]{0:T(1024)(128)(4,1)S(1)}, s32[]{:S(2)}) async-start(s8[8388608]{0:T(1024)(128)(4,1)} %bitcast.67), calls=%async_computation.2 | async-start | bytes 8388608
  319.0 111.6 %all-to-all-start = ((bf16[2,128,16,1024]{3,2,0,1:T(8,128)(2,1)}), bf16[2,128,16,1024]{3,2,0,1:T(8,128)(2,1)}, u32[]{:S(2)}, u32[]{:S(2)}) async-start(bf16[2,128,16,1024]{3,2,0,1:T(8,128)(2,1)} %copy.57), calls=%async_computation | async-start | bytes 16777216 | tf_op jit(solution)/shard_map/all_to_all | solution.py:75
  734.8 62.4 %copy-start = (s32[512,1]{0,1:T(1,128)S(1)}, s32[512,1]{0,1:T(1,128)}, u32[]{:S(2)}) copy-start(s32[512,1]{0,1:T(1,128)} %shift-left_or_fusion) | copy-start | bytes 6148
  734.8 247.8 %copy-start.2 = (pred[512,512]{1,0:T(8,128)(4,1)S(1)}, pred[512,512]{1,0:T(8,128)(4,1)}, u32[]{:S(2)}) copy-start(pred[512,512]{1,0:T(8,128)(4,1)} %iota_compare_fusion) | copy-start | bytes 786436
